TPU v7x, 128 devices: a whole 4x4x4 slice. The times are simulated.
128 devices in a mesh: row: 16 (over x, z_hi, core), col: 8 (over z_lo, y).
Axes of the slice: x: 4, y: 4, z: 4 (z_hi: 2, z_lo: 2; z = z_hi * 2 + z_lo), core: 2. Of those that a mesh axis runs over, the one named last changes fastest.
Arguments:
- thin_line_values: float32 [2048, 65536], P('row', 'col'), may hold values from 0 to 65520, as said below
- occupied_patch_flags: int32 [16, 512], P('row', 'col'), may hold values 0 or 1
- leader_vertical_patch: int32 [2], replicated, may hold values from 0 to 511, as said below
- leader_square_lines: float32 [2, 128, 65536], P(None, 'row', 'col'), may hold values from 0 to 65520, as said below
- leader_square_reciprocals: float32 [2, 128, 128], replicated, may hold values from 0 to 65520, as said below
- remaining_destination_line: int32 [2048], P('row'), may hold values from 0 to 15, as said below
- leading_square_lines: float32 [512, 65536], P('row', 'col'), may hold values from 0 to 65520, as said below
- leading_square_reciprocal: float32 [512, 512], replicated, may hold values from 0 to 65520, as said below
Outputs:
- dense_grid: float32 [4096, 65536], P('row', 'col')
Inputs may be any that keep to these rules, and one draw needn't show every extreme that they name: `leader_vertical_patch`: distinct column tiles; the last column tile is among them. `remaining_destination_line`: among the rows of one index of row no value appears more than 16 times; one value, the same for every index of row, appears exactly 16 times in each. `thin_line_values`: Integers. `leader_square_lines`: Integers. `leader_square_reciprocals`: Integers. `leading_square_lines`: Integers. `leading_square_reciprocal`: Integers.
All inputs are finite; a program needn't handle non-finite values. No bound on the sum of `occupied_patch_flags` on one device may be relied on, other than what follows from the above.
Results may differ from a plain program's by a relative error of at most 0.0003.
Values sent between devices are 32-bit elements; how exact they have to be, the bound alone decides.
A program may use at most 256 MiB of HBM per device.

v0:
```python
import jax
import jax.numpy as jnp
from jax import lax
from jax.sharding import PartitionSpec as P

TILE = 128
PANEL = 512
NPIV = 2
MAX_PER_DEST = 16
modulus = 65521.0


def broadcast(block, axis, owner):
    block = jnp.where(lax.axis_index(axis) == owner, block, jnp.zeros_like(block))
    return lax.psum(block, axis)


def reduce_mod(values):
    quotient = jnp.floor(values / modulus)
    remain = values - quotient * modulus
    remain = jnp.where(remain < 0.0, remain + modulus, remain)
    return jnp.where(remain >= modulus, remain - modulus, remain)


def split_limbs(values):
    upper = jnp.floor(values / 256.0)
    return (upper.astype(jnp.bfloat16), (values - upper * 256.0).astype(jnp.bfloat16))


def mul_mod(left, right):
    left_hi, left_lo = split_limbs(left)
    right_hi, right_lo = split_limbs(right)
    total = jnp.zeros((left.shape[0], right.shape[1]), jnp.float32)
    for offset in range(0, left.shape[1], 128):
        a_hi = left_hi[:, offset : offset + 128]
        a_lo = left_lo[:, offset : offset + 128]
        b_hi = right_hi[offset : offset + 128]
        b_lo = right_lo[offset : offset + 128]
        high = jnp.dot(a_hi, b_hi, preferred_element_type=jnp.float32)
        cross = jnp.dot(a_hi, b_lo, preferred_element_type=jnp.float32) + jnp.dot(
            a_lo, b_hi, preferred_element_type=jnp.float32
        )
        low = jnp.dot(a_lo, b_lo, preferred_element_type=jnp.float32)
        part = reduce_mod(reduce_mod(cross) * 256.0) + reduce_mod(high) * 15.0 + reduce_mod(low)
        total = reduce_mod(total + part)
    return total


def share_multiplier(values, owner):
    return broadcast(values, "col", owner)


def dispatched_lines(chain_differential, remaining_destination_line):
    outbound_lines = lax.axis_size("row")
    indicator_matrix = (
        remaining_destination_line[:, None] == jnp.arange(outbound_lines, dtype=jnp.int32)[None, :]
    ).astype(jnp.int32)
    landing_order = jnp.sum((jnp.cumsum(indicator_matrix, axis=0) - 1) * indicator_matrix, axis=1)
    incoming_places = remaining_destination_line * MAX_PER_DEST + landing_order
    outgoing = (
        jnp.zeros((outbound_lines * MAX_PER_DEST, chain_differential.shape[1]), jnp.float32)
        .at[incoming_places]
        .set(chain_differential)
    )
    return lax.all_to_all(outgoing, "row", split_axis=0, concat_axis=0, tiled=True)


def panel_step(chain_differential, leading_square_lines, leading_square_reciprocal):
    panel_terms = mul_mod(chain_differential[:, :PANEL], leading_square_reciprocal)
    lower = broadcast(panel_terms, "col", 0)
    strip = lax.all_gather(leading_square_lines, "row", axis=0, tiled=True)
    update = mul_mod(lower, strip)
    return reduce_mod(chain_differential - update) / modulus


def local(
    thin_line_values,
    occupied_patch_flags,
    leader_vertical_patch,
    leader_square_lines,
    leader_square_reciprocals,
    remaining_destination_line,
    leading_square_lines,
    leading_square_reciprocal,
):
    rows_dev, width_dev = thin_line_values.shape
    tiles_dev = width_dev // TILE
    shaped = thin_line_values.reshape(rows_dev // TILE, TILE, tiles_dev, TILE)
    shaped = shaped * occupied_patch_flags.astype(jnp.float32)[:, None, :, None]
    eliminated_lines = shaped.reshape(rows_dev, width_dev)
    for pivot in range(NPIV):
        block_rows = lax.all_gather(leader_square_lines[pivot], "row", axis=0, tiled=True)
        column = leader_vertical_patch[pivot]
        owner = column // tiles_dev
        offset = column % tiles_dev * TILE
        tile_now, owner = (lax.dynamic_slice_in_dim(eliminated_lines, offset, TILE, 1), owner)
        factor = share_multiplier(mul_mod(tile_now, leader_square_reciprocals[pivot]), owner)
        eliminated_lines = reduce_mod(eliminated_lines - mul_mod(factor, block_rows))
    patchwise_arrangement = dispatched_lines(eliminated_lines, remaining_destination_line)
    return panel_step(patchwise_arrangement, leading_square_lines, leading_square_reciprocal)


def solution(mesh):
    return jax.shard_map(
        local,
        mesh=mesh,
        in_specs=(
            P("row", "col"),
            P("row", "col"),
            P(),
            P(None, "row", "col"),
            P(),
            P("row"),
            P("row", "col"),
            P(),
        ),
        out_specs=P("row", "col"),
        check_vma=False,
    )
```

profile of v0, /device:TPU:1, one launch (start us, length us, event | category | flops | bytes accessed | tf_op | source)
XLA Modules:
  0.0 635.3 jit_solution(7856029149557377119)
XLA Ops:
  12.1 2.6 broadcast_multiply_fusion
  15.0 1.7 copy-done.3
  16.9 1.7 fusion.121
  23.2 66.9 %all-reduce.4.cloned.1.call-done = f32[128,128]{1,0:T(8,128)} async-done(((f32[128,128]{1,0:T(8,128)}), f32[128,128]{1,0:T(8,128)}) %all-reduce.4.cloned.1.call-update) | async-done | bytes 65552 | tf_op jit(solution)/shard_map/psum | solution.py:15
  90.1 3.3 fusion.167
  96.8 9.7 %compare_select_fusion.54 = f32[128,8192]{1,0:T(8,128)S(1)} fusion(f32[128,8192]{1,0:T(8,128)S(1)} %copy-done.4, f32[128,8192]{1,0:T(8,128)S(1)} %fusion.167, f32[128,8192]{1,0:T(8,128)S(1)} %fusion.70, f32[128,8192]{1,0:T(8,128)S(1)} %fusion.169, f32[1,128,8192]{2,1,0:T(8,128)S(1)} %copy-done.1, f32[128,128]{1,0:T(8,128)S(1)} %copy-done.7), kind=kOutput, calls=%fused_computation.58 | convolution fusion | flops 340869120 | bytes 25231360 | tf_op jit(solution)/shard_map/dot_general | solution.py:40
  107.0 1.6 copy-done.10
  109.5 29.2 %all-gather.10.cloned.1.call-done = f32[1,128,8192]{2,1,0:T(8,128)} async-done(((f32[1,8,8192]{2,1,0:T(8,128)}), f32[1,128,8192]{2,1,0:T(8,128)}) %all-gather.10.cloned.1.call-update) | async-done | bytes 4194320 | tf_op jit(solution)/shard_map/all_gather | solution.py:92
  138.7 42.9 %all-reduce.6.cloned.1.call-done = f32[128,128]{1,0:T(8,128)} async-done(((f32[128,128]{1,0:T(8,128)}), f32[128,128]{1,0:T(8,128)}) %all-reduce.6.cloned.1.call-update) | async-done | bytes 65552 | tf_op jit(solution)/shard_map/psum | solution.py:15
  181.6 3.2 fusion.171
  188.0 9.4 %fusion.25 = f32[128,8192]{1,0:T(8,128)} fusion(f32[128,8192]{1,0:T(8,128)S(1)} %copy-done.11, f32[128,8192]{1,0:T(8,128)S(1)} %fusion.171, f32[128,8192]{1,0:T(8,128)S(1)} %fusion.67, f32[128,8192]{1,0:T(8,128)S(1)} %fusion.173, f32[1,128,8192]{2,1,0:T(8,128)S(1)} %copy-done, f32[128,128]{1,0:T(8,128)S(1)} %copy-done.8), kind=kOutput, calls=%fused_computation.100 | convolution fusion | flops 330383360 | bytes 25231360 | tf_op jit(solution)/shard_map/dot_general | solution.py:40
  197.4 9.7 %scatter_custom_fusion = f32[256,8192]{1,0:T(8,128)} fusion(s32[128]{0:T(128)S(1)} %compare_select_fusion.127, f32[128,8192]{1,0:T(8,128)} %fusion.25, f32[]{:T(128)} %constant.215.clone.1, f32[]{:T(128)} %constant.231.clone.1, f32[]{:T(128)} %constant.230.clone.1, f32[]{:T(128)} %constant.229.clone.1), kind=kCustom, calls=%fused_computation.101 | custom fusion | flops 10485760 | bytes 12585472 | tf_op jit(solution)/shard_map/scatter | solution.py:63
  207.1 12.2 %all-to-all-start = ((f32[16,16,8192]{2,1,0:T(8,128)}), f32[16,16,8192]{2,1,0:T(8,128)}, u32[]{:S(2)}, u32[]{:S(2)}) async-start(f32[16,16,8192]{2,1,0:T(8,128)} %bitcast.69), calls=%async_computation | async-start | bytes 16777216 | tf_op jit(solution)/shard_map/all_to_all | solution.py:65
  219.5 131.2 %all-to-all-done = f32[16,16,8192]{2,1,0:T(8,128)} async-done(((f32[16,16,8192]{2,1,0:T(8,128)}), f32[16,16,8192]{2,1,0:T(8,128)}, u32[]{:S(2)}, u32[]{:S(2)}) %all-to-all-start) | async-done | bytes 8388640 | tf_op jit(solution)/shard_map/all_to_all | solution.py:65
  355.1 4.5 fusion.88
  360.2 71.5 %all-reduce.8.cloned.1.call-done = f32[256,512]{1,0:T(8,128)} async-done(((f32[256,512]{1,0:T(8,128)}), f32[256,512]{1,0:T(8,128)}) %all-reduce.8.cloned.1.call-update) | async-done | bytes 524304 | tf_op jit(solution)/shard_map/psum | solution.py:15
  432.9 48.8 %all-gather.6.cloned.1.call-done = f32[512,8192]{1,0:T(8,128)} async-done(((f32[32,8192]{1,0:T(8,128)}), f32[512,8192]{1,0:T(8,128)}) %all-gather.6.cloned.1.call-update) | async-done | bytes 16777232 | tf_op jit(solution)/shard_map/all_gather | solution.py:71
  481.6 7.9 %subtract_convert_fusion = (bf16[512,8192]{1,0:T(8,128)(2,1)S(1)}, bf16[512,8192]{1,0:T(8,128)(2,1)S(1)}) fusion(f32[512,8192]{1,0:T(8,128)} %all-gather.6.cloned.1.call-done), kind=kLoop, calls=%fused_computation.43 | loop fusion | flops 25165824 | bytes 33554432 | tf_op jit(solution)/shard_map/convert_element_type | solution.py:27
  489.5 4.5 fusion.62
  494.0 4.5 fusion.55
  498.4 4.5 fusion.48
  502.9 4.5 fusion.59
  507.4 4.5 fusion.52
  511.9 4.5 fusion.45
  516.3 4.6 fusion.39
  521.0 4.5 fusion.43
  525.4 4.5 fusion.50
  532.7 8.0 %convolution_add_fusion = f32[256,8192]{1,0:T(8,128)} fusion(f32[256,8192]{1,0:T(8,128)} %fusion.43, bf16[512,8192]{1,0:T(8,128)(2,1)S(1)} %get-tuple-element.6, bf16[256,512]{1,0:T(8,128)(2,1)S(1)} %get-tuple-element.11), kind=kOutput, calls=%fused_computation.70 | convolution fusion | flops 538968064 | bytes 18939904 | tf_op jit(solution)/shard_map/dot_general | solution.py:40
  540.7 8.1 %convolution_add_fusion.1 = f32[256,8192]{1,0:T(8,128)} fusion(f32[256,8192]{1,0:T(8,128)} %fusion.50, bf16[512,8192]{1,0:T(8,128)(2,1)S(1)} %get-tuple-element.6, bf16[256,512]{1,0:T(8,128)(2,1)S(1)} %get-tuple-element.11), kind=kOutput, calls=%fused_computation.71 | convolution fusion | flops 538968064 | bytes 18939904 | tf_op jit(solution)/shard_map/dot_general | solution.py:40
  548.9 4.5 convolution_add_fusion.2
  553.3 5.4 convolution_add_fusion.3
  559.5 68.0 %fusion.17 = f32[256,8192]{1,0:T(8,128)} fusion(f32[256,8192]{1,0:T(8,128)} %bitcast.9, f32[256,8192]{1,0:T(8,128)} %fusion.39, f32[256,8192]{1,0:T(8,128)} %convolution_add_fusion, f32[256,8192]{1,0:T(8,128)} %fusion.48, f32[256,8192]{1,0:T(8,128)} %fusion.45, f32[256,8192]{1,0:T(8,128)S(1)} %copy-done.2, f32[256,8192]{1,0:T(8,128)} %fusion.55, ...), kind=kOutput, calls=%fused_computation.92 | convolution fusion | flops 1021313024 | bytes 111214592 | tf_op jit(solution)/shard_map/dot_general | solution.py:43
  (76 shorter events, 22.0 us)
Async XLA Ops:
  7.4 82.8 %all-reduce.4.cloned.1.call-start = ((), (), s32[]{:S(2)}) async-start(), calls=%async_computation.1 | async-start | bytes 131072 | tf_op jit(solution)/shard_map/psum | solution.py:15
  12.1 2.7 copy-start.5
  12.1 6.6 %copy-start.9 = (f32[2,8,8192]{2,1,0:T(8,128)S(1)}, f32[2,8,8192]{2,1,0:T(8,128)}, u32[]{:S(2)}) copy-start(f32[2,8,8192]{2,1,0:T(8,128)} %param.11) | copy-start | bytes 1572868
  12.1 10.7 %copy-start.12 = (s32[128]{0:T(128)S(1)}, s32[128]{0:T(128)}, u32[]{:S(2)}) copy-start(s32[128]{0:T(128)} %param.13) | copy-start | bytes 1540
  14.7 2.0 copy-start.3
  18.6 71.5 %all-gather.8.cloned.1.call-start = ((), (), s32[]{:S(2)}) async-start(), calls=%async_computation.5 | async-start | bytes 4456448 | tf_op jit(solution)/shard_map/all_gather | solution.py:92
  19.6 119.1 %all-gather.10.cloned.1.call-start = ((), (), s32[]{:S(2)}) async-start(), calls=%async_computation.6 | async-start | bytes 4456448 | tf_op jit(solution)/shard_map/all_gather | solution.py:92
  20.2 161.4 %all-reduce.6.cloned.1.call-start = ((), (), s32[]{:S(2)}) async-start(), calls=%async_computation.2 | async-start | bytes 131072 | tf_op jit(solution)/shard_map/psum | solution.py:15
  90.1 3.3 copy-start.7
  90.1 3.8 copy-start.1
  94.6 2.2 copy-start.4
  106.6 2.0 copy-start.10
  181.6 3.5 copy-start
  181.6 3.5 copy-start.8
  185.8 2.2 copy-start.11
  207.1 12.2 %copy-start.6 = (f32[512,512]{1,0:T(8,128)S(1)}, f32[512,512]{1,0:T(8,128)}, u32[]{:S(2)}) copy-start(f32[512,512]{1,0:T(8,128)} %param.15) | copy-start | bytes 3145732
  207.1 143.7 %all-to-all-start = ((f32[16,16,8192]{2,1,0:T(8,128)}), f32[16,16,8192]{2,1,0:T(8,128)}, u32[]{:S(2)}, u32[]{:S(2)}) async-start(f32[16,16,8192]{2,1,0:T(8,128)} %bitcast.69), calls=%async_computation | async-start | bytes 16777216 | tf_op jit(solution)/shard_map/all_to_all | solution.py:65
  219.3 212.4 %all-reduce.8.cloned.1.call-start = ((), (), s32[]{:S(2)}) async-start(), calls=%async_computation.3 | async-start | bytes 1048576 | tf_op jit(solution)/shard_map/psum | solution.py:15
  359.6 122.0 %all-gather.6.cloned.1.call-start = ((), (), s32[]{:S(2)}) async-start(), calls=%async_computation.4 | async-start | bytes 17825792 | tf_op jit(solution)/shard_map/all_gather | solution.py:71
  553.3 6.2 copy-start.2
Sparse Core Ops, SparseCore 0:
  18.8 71.3 all-reduce.3
  109.6 71.9 all-reduce.5
  359.8 71.9 all-reduce.7
Sparse Core Ops, SparseCore 1:
  21.5 59.7 all-gather.7
  83.9 54.8 all-gather.9
  362.5 119.1 all-gather.5
where the time goes:
time: 645 us; the launch traced here: 635 us
  waiting for transfers between devices  392 us (61%)
  matrix products  177 us (27%)
  other arithmetic  23.8 us (4%)
  between operations  20.7 us (3%)
  starting transfers between devices  12.4 us (2%)
  local copies, waits for them, and re-layouts  9.99 us (2%)
    psum x3, waiting for transfers between devices, broadcast(): return lax.psum(block, axis)  181 us
    all_to_all x1, waiting for transfers between devices, dispatched_lines(): lax.all_to_all(outgoing, 'row', split_axis=0, concat_axis=0, tiled=True)  131 us
    dot_general x12, matrix products, mul_mod(): low = jnp.dot(a_lo, b_lo, preferred_element_type=jnp.float32)  93.3 us
    all_gather x1, waiting for transfers between devices, panel_step(): strip = lax.all_gather(leading_square_lines, 'row', axis=0, tiled=True)  48.8 us
    dot_general x12, matrix products, mul_mod(): jnp.dot(a_lo, b_hi, preferred_element_type=jnp.float32)  48.5 us
    all_gather x2, waiting for transfers between devices, local(): lax.all_gather(leader_square_lines[pivot], 'row', axis=0, tiled=True)  29.2 us
    dot_general x12, matrix products, mul_mod(): high = jnp.dot(a_hi, b_hi, preferred_element_type=jnp.float32)  20.5 us
    dot_general x12, matrix products, mul_mod(): jnp.dot(a_hi, b_lo, preferred_element_type=jnp.float32)  14.4 us
  transfers between devices with their start and end apart: 7, of which 6 were waited for; matrix products, arithmetic and copies ran while one was open for 3% of the time, Pallas kernels for 0%

commit v1 on v0

--- a/solution.py
+++ b/solution.py
@@ -89,7 +89,12 @@
     shaped = shaped * occupied_patch_flags.astype(jnp.float32)[:, None, :, None]
     eliminated_lines = shaped.reshape(rows_dev, width_dev)
     for pivot in range(NPIV):
-        block_rows = lax.all_gather(leader_square_lines[pivot], "row", axis=0, tiled=True)
+        block_rows = jnp.concatenate(
+            lax.all_to_all(
+                jnp.stack([leader_square_lines[pivot]] * lax.axis_size("row")), "row", 0, 0
+            ),
+            axis=0,
+        )
         column = leader_vertical_patch[pivot]
         owner = column // tiles_dev
         offset = column % tiles_dev * TILE

time: 645 us -> 672 us (1.042)
  starting transfers between devices: 12.4 us -> 45.7 us
  waiting for transfers between devices: 392 us -> 379 us
  matrix products: 177 us -> 188 us
    all_to_all x0 -> x2, waiting for transfers between devices: none -> 58 us  [local(): lax.all_to_all(jnp.stack([leader_square_lines[pivot]] * lax.axis_size('ro...]
    psum x3, waiting for transfers between devices: 181 us -> 141 us  [broadcast(): return lax.psum(block, axis)]
    all_gather x2 -> x0, waiting for transfers between devices: 29.2 us -> none  [local(): lax.all_gather(leader_square_lines[pivot], 'row', axis=0, tiled=True)]
    all_to_all x0 -> x2, starting transfers between devices: none -> 21.8 us  [local(): lax.all_to_all(jnp.stack([leader_square_lines[pivot]] * lax.axis_size('ro...]
    all_to_all x1, starting transfers between devices: 12.2 us -> 23.7 us  [dispatched_lines(): lax.all_to_all(outgoing, 'row', split_axis=0, concat_axis=0, tiled=True)]
  transfers between devices with their start and end apart: 7 -> 7, of which waited for: 6 -> 7; matrix products, arithmetic and copies ran while one was open for 3% -> 5% of each run, Pallas kernels for 0% -> 0%
where the time goes in v1:
time: 672 us; the launch traced here: 667 us
  waiting for transfers between devices  379 us (56%)
  matrix products  188 us (28%)
  starting transfers between devices  45.7 us (7%)
  other arithmetic  22.9 us (3%)
  between operations  20.3 us (3%)
  local copies, waits for them, and re-layouts  11.1 us (2%)
    psum x3, waiting for transfers between devices, broadcast(): return lax.psum(block, axis)  141 us
    all_to_all x1, waiting for transfers between devices, dispatched_lines(): lax.all_to_all(outgoing, 'row', split_axis=0, concat_axis=0, tiled=True)  131 us
    dot_general x12, matrix products, mul_mod(): low = jnp.dot(a_lo, b_lo, preferred_element_type=jnp.float32)  93 us
    all_to_all x2, waiting for transfers between devices, local(): lax.all_to_all(jnp.stack([leader_square_lines[pivot]] * lax.axis_size('ro...  58 us
    dot_general x12, matrix products, mul_mod(): jnp.dot(a_lo, b_hi, preferred_element_type=jnp.float32)  50.8 us
    all_gather x1, waiting for transfers between devices, panel_step(): strip = lax.all_gather(leading_square_lines, 'row', axis=0, tiled=True)  48.9 us
    dot_general x12, matrix products, mul_mod(): high = jnp.dot(a_hi, b_hi, preferred_element_type=jnp.float32)  25 us
    all_to_all x1, starting transfers between devices, dispatched_lines(): lax.all_to_all(outgoing, 'row', split_axis=0, concat_axis=0, tiled=True)  23.7 us
  transfers between devices with their start and end apart: 7, of which 7 were waited for; matrix products, arithmetic and copies ran while one was open for 5% of the time, Pallas kernels for 0%

profile of v1, /device:TPU:1, one launch (start us, length us, event | category | flops | bytes accessed | tf_op | source)
XLA Modules:
  0.0 666.9 jit_solution(5476502917689073230)
XLA Ops:
  10.8 9.3 %all-to-all-start = ((f32[16,8,8192]{2,1,0:T(8,128)}), f32[16,8,8192]{2,1,0:T(8,128)}, u32[]{:S(2)}, u32[]{:S(2)}) async-start(f32[16,8,8192]{2,1,0:T(8,128)} %stack.6), calls=%async_computation | async-start | bytes 8388608 | tf_op jit(solution)/shard_map/all_to_all | solution.py:93
  32.0 41.7 %all-to-all-done = f32[16,8,8192]{2,1,0:T(8,128)} async-done(((f32[16,8,8192]{2,1,0:T(8,128)}), f32[16,8,8192]{2,1,0:T(8,128)}, u32[]{:S(2)}, u32[]{:S(2)}) %all-to-all-start) | async-done | bytes 4194336 | tf_op jit(solution)/shard_map/all_to_all | solution.py:93
  76.0 12.5 %all-to-all-start.1 = ((f32[16,8,8192]{2,1,0:T(8,128)}), f32[16,8,8192]{2,1,0:T(8,128)}, u32[]{:S(2)}, u32[]{:S(2)}) async-start(f32[16,8,8192]{2,1,0:T(8,128)} %stack.7), calls=%async_computation.1 | async-start | bytes 8388608 | tf_op jit(solution)/shard_map/all_to_all | solution.py:93
  88.6 12.5 %all-reduce.4.cloned.1.call-done = f32[128,128]{1,0:T(8,128)} async-done(((f32[128,128]{1,0:T(8,128)}), f32[128,128]{1,0:T(8,128)}) %all-reduce.4.cloned.1.call-update) | async-done | bytes 65552 | tf_op jit(solution)/shard_map/psum | solution.py:15
  101.1 3.1 fusion.167
  107.1 3.1 fusion.169
  110.5 11.4 %compare_select_fusion.54 = f32[128,8192]{1,0:T(8,128)S(1)} fusion(f32[128,8192]{1,0:T(8,128)S(1)} %copy-done.2, f32[128,8192]{1,0:T(8,128)S(1)} %fusion.167, f32[128,8192]{1,0:T(8,128)S(1)} %fusion.70, f32[128,8192]{1,0:T(8,128)S(1)} %fusion.169, f32[16,8,8192]{2,1,0:T(8,128)} %all-to-all-done, f32[128,128]{1,0:T(8,128)S(1)} %copy-done.5), kind=kOutput, calls=%fused_computation.58 | convolution fusion | flops 340869120 | bytes 25231360 | tf_op jit(solution)/shard_map/dot_general | solution.py:40
  124.8 16.4 %all-to-all-done.1 = f32[16,8,8192]{2,1,0:T(8,128)} async-done(((f32[16,8,8192]{2,1,0:T(8,128)}), f32[16,8,8192]{2,1,0:T(8,128)}, u32[]{:S(2)}, u32[]{:S(2)}) %all-to-all-start.1) | async-done | bytes 4194336 | tf_op jit(solution)/shard_map/all_to_all | solution.py:93
  141.2 56.6 %all-reduce.6.cloned.1.call-done = f32[128,128]{1,0:T(8,128)} async-done(((f32[128,128]{1,0:T(8,128)}), f32[128,128]{1,0:T(8,128)}) %all-reduce.6.cloned.1.call-update) | async-done | bytes 65552 | tf_op jit(solution)/shard_map/psum | solution.py:15
  203.8 3.1 fusion.173
  207.3 10.9 %fusion.25 = f32[128,8192]{1,0:T(8,128)} fusion(f32[128,8192]{1,0:T(8,128)S(1)} %copy-done.8, f32[128,8192]{1,0:T(8,128)S(1)} %fusion.171, f32[128,8192]{1,0:T(8,128)S(1)} %fusion.67, f32[128,8192]{1,0:T(8,128)S(1)} %fusion.173, f32[16,8,8192]{2,1,0:T(8,128)} %all-to-all-done.1, f32[128,128]{1,0:T(8,128)S(1)} %copy-done.6), kind=kOutput, calls=%fused_computation.100 | convolution fusion | flops 330383360 | bytes 25231360 | tf_op jit(solution)/shard_map/dot_general | solution.py:40
  218.1 9.7 %scatter_custom_fusion = f32[256,8192]{1,0:T(8,128)} fusion(s32[128]{0:T(128)S(1)} %compare_select_fusion.127, f32[128,8192]{1,0:T(8,128)} %fusion.25, f32[]{:T(128)} %constant.215.clone.1, f32[]{:T(128)} %constant.231.clone.1, f32[]{:T(128)} %constant.230.clone.1, f32[]{:T(128)} %constant.229.clone.1), kind=kCustom, calls=%fused_computation.101 | custom fusion | flops 10485760 | bytes 12585472 | tf_op jit(solution)/shard_map/scatter | solution.py:63
  227.8 23.7 %all-to-all-start.2 = ((f32[16,16,8192]{2,1,0:T(8,128)}), f32[16,16,8192]{2,1,0:T(8,128)}, u32[]{:S(2)}, u32[]{:S(2)}) async-start(f32[16,16,8192]{2,1,0:T(8,128)} %bitcast.73), calls=%async_computation.2 | async-start | bytes 16777216 | tf_op jit(solution)/shard_map/all_to_all | solution.py:65
  251.8 130.7 %all-to-all-done.2 = f32[16,16,8192]{2,1,0:T(8,128)} async-done(((f32[16,16,8192]{2,1,0:T(8,128)}), f32[16,16,8192]{2,1,0:T(8,128)}, u32[]{:S(2)}, u32[]{:S(2)}) %all-to-all-start.2) | async-done | bytes 8388640 | tf_op jit(solution)/shard_map/all_to_all | solution.py:65
  386.9 4.5 fusion.88
  392.0 71.9 %all-reduce.8.cloned.1.call-done = f32[256,512]{1,0:T(8,128)} async-done(((f32[256,512]{1,0:T(8,128)}), f32[256,512]{1,0:T(8,128)}) %all-reduce.8.cloned.1.call-update) | async-done | bytes 524304 | tf_op jit(solution)/shard_map/psum | solution.py:15
  465.0 48.9 %all-gather.2.cloned.1.call-done = f32[512,8192]{1,0:T(8,128)} async-done(((f32[32,8192]{1,0:T(8,128)}), f32[512,8192]{1,0:T(8,128)}) %all-gather.2.cloned.1.call-update) | async-done | bytes 16777232 | tf_op jit(solution)/shard_map/all_gather | solution.py:71
  513.9 7.6 %subtract_convert_fusion = (bf16[512,8192]{1,0:T(8,128)(2,1)S(1)}, bf16[512,8192]{1,0:T(8,128)(2,1)S(1)}) fusion(f32[512,8192]{1,0:T(8,128)} %all-gather.2.cloned.1.call-done), kind=kLoop, calls=%fused_computation.43 | loop fusion | flops 25165824 | bytes 33554432 | tf_op jit(solution)/shard_map/convert_element_type | solution.py:27
  521.6 4.5 fusion.62
  526.0 4.5 fusion.55
  530.5 4.5 fusion.48
  535.0 4.5 fusion.59
  539.5 4.5 fusion.52
  543.9 4.5 fusion.45
  548.4 4.6 fusion.39
  553.0 4.5 fusion.43
  557.5 4.6 fusion.50
  564.7 8.0 %convolution_add_fusion = f32[256,8192]{1,0:T(8,128)} fusion(f32[256,8192]{1,0:T(8,128)} %fusion.43, bf16[512,8192]{1,0:T(8,128)(2,1)S(1)} %get-tuple-element.6, bf16[256,512]{1,0:T(8,128)(2,1)S(1)} %get-tuple-element.11), kind=kOutput, calls=%fused_computation.70 | convolution fusion | flops 538968064 | bytes 18939904 | tf_op jit(solution)/shard_map/dot_general | solution.py:40
  572.8 8.1 %convolution_add_fusion.1 = f32[256,8192]{1,0:T(8,128)} fusion(f32[256,8192]{1,0:T(8,128)} %fusion.50, bf16[512,8192]{1,0:T(8,128)(2,1)S(1)} %get-tuple-element.6, bf16[256,512]{1,0:T(8,128)(2,1)S(1)} %get-tuple-element.11), kind=kOutput, calls=%fused_computation.71 | convolution fusion | flops 538968064 | bytes 18939904 | tf_op jit(solution)/shard_map/dot_general | solution.py:40
  580.9 4.5 convolution_add_fusion.2
  585.4 5.4 convolution_add_fusion.3
  591.6 68.0 %fusion.17 = f32[256,8192]{1,0:T(8,128)} fusion(f32[256,8192]{1,0:T(8,128)} %bitcast.11, f32[256,8192]{1,0:T(8,128)} %fusion.39, f32[256,8192]{1,0:T(8,128)} %convolution_add_fusion, f32[256,8192]{1,0:T(8,128)} %fusion.48, f32[256,8192]{1,0:T(8,128)} %fusion.45, f32[256,8192]{1,0:T(8,128)S(1)} %copy-done, f32[256,8192]{1,0:T(8,128)} %fusion.55, ...), kind=kOutput, calls=%fused_computation.92 | convolution fusion | flops 1021313024 | bytes 111214592 | tf_op jit(solution)/shard_map/dot_general | solution.py:43
  (74 shorter events, 34.5 us)
Async XLA Ops:
  10.8 9.3 %copy-start.10 = (s32[2]{0:T(128)S(1)}, s32[2]{0:T(128)}, u32[]{:S(2)}) copy-start(s32[2]{0:T(128)} %param.10) | copy-start | bytes 28
  10.8 12.5 %copy-start.11 = (s32[1,64]{1,0:T(1,128)S(1)}, s32[1,64]{1,0:T(1,128)}, u32[]{:S(2)}) copy-start(s32[1,64]{1,0:T(1,128)} %param.9) | copy-start | bytes 772
  10.8 62.8 %all-to-all-start = ((f32[16,8,8192]{2,1,0:T(8,128)}), f32[16,8,8192]{2,1,0:T(8,128)}, u32[]{:S(2)}, u32[]{:S(2)}) async-start(f32[16,8,8192]{2,1,0:T(8,128)} %stack.6), calls=%async_computation | async-start | bytes 8388608 | tf_op jit(solution)/shard_map/all_to_all | solution.py:93
  20.1 81.0 %all-reduce.4.cloned.1.call-start = ((), (), s32[]{:S(2)}) async-start(), calls=%async_computation.3 | async-start | bytes 131072 | tf_op jit(solution)/shard_map/psum | solution.py:15
  23.5 2.6 copy-start.3
  23.5 8.1 %copy-start.9 = (s32[128]{0:T(128)S(1)}, s32[128]{0:T(128)}, u32[]{:S(2)}) copy-start(s32[128]{0:T(128)} %param.13) | copy-start | bytes 1540
  26.1 2.0 copy-start.1
  76.0 65.2 %all-to-all-start.1 = ((f32[16,8,8192]{2,1,0:T(8,128)}), f32[16,8,8192]{2,1,0:T(8,128)}, u32[]{:S(2)}, u32[]{:S(2)}) async-start(f32[16,8,8192]{2,1,0:T(8,128)} %stack.7), calls=%async_computation.1 | async-start | bytes 8388608 | tf_op jit(solution)/shard_map/all_to_all | solution.py:93
  88.6 109.3 %all-reduce.6.cloned.1.call-start = ((), (), s32[]{:S(2)}) async-start(), calls=%async_computation.4 | async-start | bytes 131072 | tf_op jit(solution)/shard_map/psum | solution.py:15
  101.1 3.1 copy-start.5
  107.1 3.5 copy-start.2
  121.9 2.0 copy-start.7
  197.8 3.1 copy-start.6
  203.8 3.5 copy-start.8
  227.8 23.8 %copy-start.4 = (f32[512,512]{1,0:T(8,128)S(1)}, f32[512,512]{1,0:T(8,128)}, u32[]{:S(2)}) copy-start(f32[512,512]{1,0:T(8,128)} %param.15) | copy-start | bytes 3145732
  227.8 154.7 %all-to-all-start.2 = ((f32[16,16,8192]{2,1,0:T(8,128)}), f32[16,16,8192]{2,1,0:T(8,128)}, u32[]{:S(2)}, u32[]{:S(2)}) async-start(f32[16,16,8192]{2,1,0:T(8,128)} %bitcast.73), calls=%async_computation.2 | async-start | bytes 16777216 | tf_op jit(solution)/shard_map/all_to_all | solution.py:65
  251.6 212.3 %all-reduce.8.cloned.1.call-start = ((), (), s32[]{:S(2)}) async-start(), calls=%async_computation.5 | async-start | bytes 1048576 | tf_op jit(solution)/shard_map/psum | solution.py:15
  391.4 122.5 %all-gather.2.cloned.1.call-start = ((), (), s32[]{:S(2)}) async-start(), calls=%async_computation.6 | async-start | bytes 17825792 | tf_op jit(solution)/shard_map/all_gather | solution.py:71
  585.4 6.2 copy-start
Sparse Core Ops, SparseCore 0:
  29.1 71.9 all-reduce.3
  125.0 72.8 all-reduce.5
  391.5 72.2 all-reduce.7
Sparse Core Ops, SparseCore 1:
  394.3 119.5 all-gather.1
